TPU v7x, 32 devices: a whole 2x2x4 slice. The times are simulated.
32 devices in a mesh: grp: 2 (over y), ctx: 4 (over z), ch: 4 (over x, core).
Axes of the slice: x: 2, y: 2, z: 4, core: 2. Of those that a mesh axis runs over, the one named last changes fastest.
Arguments:
- fwd_hidden: bfloat16 [4096, 2048], P(('grp', 'ctx'), 'ch'), parts along dimension 0, may hold values from -6 to 6
- rev_hidden: bfloat16 [4096, 2048], P(('grp', 'ctx'), 'ch'), parts along dimension 0, may hold values from -6 to 6
- bases: int32 [4096], P(('grp', 'ctx')), parts along dimension 0, may hold values from 0 to 3
- complement: int32 [4], replicated, may hold values from 0 to 3, each once
- offsets: int32 [32], P('grp'), parts along dimension 0, may hold values from 0 to 2047, as said below
- base_embed: bfloat16 [4, 2048], P(None, 'ch'), may hold values from -6 to 6
- norm_gain: float32 [2048], replicated, may hold values from 0.1 to 1.9
- in_weight: bfloat16 [4, 2048, 2048], P(None, 'ctx', 'ch'), may hold values from -0.125 to 0.125
- filters: float32 [3, 16, 128], P(None, 'ch'), may hold values from -0.5 to 0.5
- out_weight: bfloat16 [2048, 2048], P('ctx', 'ch'), may hold values from -0.125 to 0.125
Outputs:
- block_out: bfloat16 [4096, 2048], P(('grp', 'ctx'), 'ch'), parts along dimension 0
There are 2 independent parts, one for each index of `grp`. A program takes and returns all parts, laid end to end along the dimension named above; an argument that names none is the same for every part. Nothing has to cross between parts.
Inputs may be any that keep to these rules, and one draw needn't show every extreme that they name: The first offset is 0, the last is 2047, and the offsets rise strictly; each is the first position of a document. `complement`: A permutation of the 4 letters.
All inputs are finite; a program needn't handle non-finite values.
Results may differ from a plain program's by a relative error of at most 0.012.
Values may be sent and summed in bfloat16 or wider, within the bound.
No kernel may reach another device: no remote copies, remote signals or barrier semaphores. Data moves between devices by JAX's collectives and lax.ppermute only.
A program may use at most 64 MiB of HBM per device.

v0:
```python
import jax
import jax.numpy as jnp
from jax import lax
from jax.sharding import PartitionSpec as P


def partner(block, axis, apart):
    count = lax.axis_size(axis)
    route = []
    for low in range(count):
        high = low | 1 << apart
        if high != low and high < count:
            route += [(low, high), (high, low)]
    return lax.ppermute(block, axis, route)


def shifted(value, axis, by):
    count = lax.axis_size(axis)
    pairs = [(i, i + by) for i in range(count) if 0 <= i + by < count]
    return lax.ppermute(value, axis, pairs)


def doc_of(positions, offsets, seq_len):
    count = jnp.sum((offsets[None, :] <= positions[:, None]).astype(jnp.int32), axis=1) - 1
    inside = (positions >= 0) & (positions < seq_len)
    return jnp.where(inside, count, -1)


def toeplitz(taps):
    heads, block = taps.shape
    pattern = jnp.concatenate(
        [jnp.zeros((heads, 1), taps.dtype), taps[:, ::-1], jnp.zeros((heads, block), taps.dtype)],
        axis=1,
    )
    repeated = jnp.tile(pattern, (1, block))
    return repeated[:, : block * 2 * block].reshape(heads, block, 2 * block)


def rms_norm(values, gain):
    floats = values.astype(jnp.float32)
    scale = lax.rsqrt(jnp.mean(floats * floats, axis=-1, keepdims=True) + 1e-05)
    return (floats * scale * gain).astype(jnp.bfloat16)


def blockwise_conv(conv_in, rim, taps, ext_docs):
    rows, width = conv_in.shape
    heads, block = taps.shape
    head_dim = width // heads
    blocks = rows // block
    extended = jnp.concatenate([rim, conv_in], axis=0)
    target_docs = ext_docs[block:].reshape(blocks, block)
    window = jnp.concatenate(
        [
            extended[:rows].reshape(blocks, block, width),
            extended[block:].reshape(blocks, block, width),
        ],
        axis=1,
    )
    window = window.reshape(blocks, 2 * block, heads, head_dim)
    window_docs = jnp.concatenate(
        [ext_docs[:rows].reshape(blocks, block), ext_docs[block:].reshape(blocks, block)], axis=1
    )
    mask = (target_docs[:, :, None] == window_docs[:, None, :]).astype(jnp.bfloat16)
    kernel = toeplitz(taps)[None] * mask[:, None]
    result = jnp.einsum("nhts,nshd->nthd", kernel, window, preferred_element_type=jnp.float32)
    return result.reshape(rows, width)


def local(
    fwd_hidden,
    rev_hidden,
    bases,
    complement,
    offsets,
    base_embed,
    norm_gain,
    in_weight,
    filters,
    out_weight,
):
    rows, width_local = fwd_hidden.shape
    ctx_count = lax.axis_size("ctx")
    here = lax.axis_index("ctx")
    seq_len = rows * ctx_count
    letters = base_embed.shape[0]
    alphabet = jnp.arange(letters, dtype=jnp.int32)
    onehot = (bases[:, None] == alphabet[None, :]).astype(jnp.bfloat16)
    swap_table = (complement[:, None] == alphabet[None, :]).astype(jnp.bfloat16)
    onehot_rev = jnp.dot(onehot, swap_table, preferred_element_type=jnp.float32).astype(
        jnp.bfloat16
    )
    embed_fwd = jnp.dot(onehot, base_embed, preferred_element_type=jnp.float32)
    embed_rev = jnp.dot(onehot_rev, base_embed, preferred_element_type=jnp.float32)
    fwd_input = (fwd_hidden.astype(jnp.float32) + embed_fwd).astype(jnp.bfloat16)
    rev_input = (rev_hidden.astype(jnp.float32) + embed_rev).astype(jnp.bfloat16)
    levels = ctx_count.bit_length() - 1
    for level in range(levels):
        rev_input = partner(rev_input, "ctx", level)
    rev_input = rev_input[::-1]
    full_fwd, full_rev = (
        lax.all_gather(fwd_input, "ch", axis=1, tiled=True),
        lax.all_gather(rev_input, "ch", axis=1, tiled=True),
    )
    normed_fwd = rms_norm(full_fwd, norm_gain)
    normed_rev = rms_norm(full_rev, norm_gain)
    piece = lax.all_gather(in_weight, "ctx", axis=1, tiled=True)
    add_fwd = jnp.einsum("rd,bdc->brc", normed_fwd, piece, preferred_element_type=jnp.float32)
    add_rev = jnp.einsum("rd,bdc->brc", normed_rev, piece, preferred_element_type=jnp.float32)
    taps_all = filters.astype(jnp.bfloat16)
    block = filters.shape[-1]
    before = here * rows - block + jnp.arange(rows + block, dtype=jnp.int32)
    docs_fwd = doc_of(before, offsets, seq_len)
    docs_rev = doc_of(seq_len - 1 - before, offsets, seq_len)
    state_fwd = add_fwd[0]
    state_rev = add_rev[0]
    for section in range(filters.shape[0]):
        in_fwd = state_fwd.astype(jnp.bfloat16)
        in_rev = state_rev.astype(jnp.bfloat16)
        rim_fwd, rim_rev = shifted((in_fwd[-block:], in_rev[-block:]), "ctx", 1)
        conv_rev = blockwise_conv(in_rev, rim_rev, taps_all[section], docs_rev)
        conv_fwd = blockwise_conv(in_fwd, rim_fwd, taps_all[section], docs_fwd)
        state_fwd = add_fwd[section + 1] * conv_fwd
        state_rev = add_rev[section + 1] * conv_rev
    mixed_fwd = state_fwd.astype(jnp.bfloat16)
    mixed_rev = state_rev.astype(jnp.bfloat16)
    for level in range(levels):
        mixed_rev = partner(mixed_rev, "ctx", level)
    mixed_rev = mixed_rev[::-1]
    mixed_sum = (mixed_fwd.astype(jnp.float32) + mixed_rev.astype(jnp.float32)).astype(jnp.bfloat16)
    whole_sum = lax.all_gather(mixed_sum, "ch", axis=1, tiled=True)
    total = jnp.dot(
        whole_sum,
        lax.all_gather(out_weight, "ctx", axis=0, tiled=True),
        preferred_element_type=jnp.float32,
    )
    return total.astype(jnp.bfloat16)


def solution(mesh):
    in_specs = (
        P(("grp", "ctx"), "ch"),
        P(("grp", "ctx"), "ch"),
        P(("grp", "ctx")),
        P(),
        P("grp"),
        P(None, "ch"),
        P(),
        P(None, "ctx", "ch"),
        P(None, "ch", None),
        P("ctx", "ch"),
    )
    out_specs = P(("grp", "ctx"), "ch")
    return jax.shard_map(local, mesh=mesh, in_specs=in_specs, out_specs=out_specs, check_vma=False)
```

profile of v0, /device:TPU:0, one launch (start us, length us, event | category | flops | bytes accessed | tf_op | source)
XLA Modules:
  0.0 390.4 jit_solution(10410948972962377146)
XLA Ops:
  7.2 2.2 fusion.14
  9.5 1.7 fusion.15
  11.2 3.1 collective-permute-start.3
  14.3 11.9 %collective-permute-done.3 = bf16[512,512]{1,0:T(8,128)(2,1)S(1)} collective-permute-done((bf16[512,512]{1,0:T(8,128)(2,1)S(1)}, bf16[512,512]{1,0:T(8,128)(2,1)S(1)}, u32[]{:S(2)}, u32[]{:S(2)}) %collective-permute-start.3) | collective-permute-done | bytes 524320 | tf_op jit(solution)/shard_map/ppermute | solution.py:14
  26.2 2.8 collective-permute-start.4
  28.9 22.6 %collective-permute-done.4 = bf16[512,512]{1,0:T(8,128)(2,1)S(1)} collective-permute-done((bf16[512,512]{1,0:T(8,128)(2,1)S(1)}, bf16[512,512]{1,0:T(8,128)(2,1)S(1)}, u32[]{:S(2)}, u32[]{:S(2)}) %collective-permute-start.4) | collective-permute-done | bytes 524320 | tf_op jit(solution)/shard_map/ppermute | solution.py:14
  51.5 5.1 %rev.21 = bf16[512,512]{1,0:T(8,128)(2,1)} reverse(bf16[512,512]{1,0:T(8,128)(2,1)S(1)} %collective-permute-done.4), dimensions={0} | reverse | bytes 1048576 | tf_op jit(solution)/shard_map/rev | solution.py:99
  58.8 0.8 tile.13
  60.4 0.8 tile.15
  62.1 0.8 tile.17
  63.7 0.8 compare_convert_fusion
  64.7 2.4 fusion
  67.1 13.3 %all-gather.10.cloned.1.call-done = bf16[512,2048]{1,0:T(8,128)(2,1)} async-done(((bf16[512,512]{1,0:T(8,128)(2,1)}), bf16[512,2048]{1,0:T(8,128)(2,1)}) %all-gather.10.cloned.1.call-update) | async-done | bytes 2097168 | tf_op jit(solution)/shard_map/all_gather | solution.py:102
  80.4 2.2 fusion.3
  82.6 149.0 %all-gather.8.cloned.1.call-done = bf16[4,2048,512]{2,1,0:T(8,128)(2,1)} async-done(((bf16[4,512,512]{2,1,0:T(8,128)(2,1)}), bf16[4,2048,512]{2,1,0:T(8,128)(2,1)}) %all-gather.8.cloned.1.call-update) | async-done | bytes 8388624 | tf_op jit(solution)/shard_map/all_gather | solution.py:106
  231.7 7.1 %convolution_bitcast_fusion = f32[4,512,512]{2,1,0:T(8,128)S(1)} fusion(bf16[4,2048,512]{2,1,0:T(8,128)(2,1)} %all-gather.8.cloned.1.call-done, bf16[512,2048]{1,0:T(8,128)(2,1)S(1)} %copy-done.10, f32[512]{0:T(512)S(1)} %add_rsqrt_fusion, f32[2048]{0:T(1024)S(1)} %copy-done.14), kind=kOutput, calls=%fused_computation.10 | convolution fusion | flops 4299161600 | bytes 14690304 | tf_op jit(solution)/shard_map/rd,bdc->brc/dot_general | solution.py:108
  238.8 1.3 fusion.88
  240.1 1.0 copy-done.3
  241.1 0.8 slice_bitcast_fusion.10
  241.9 0.9 convert_element_type.147
  243.5 7.7 %convolution_bitcast_fusion.1 = f32[4,512,512]{2,1,0:T(8,128)S(1)} fusion(bf16[4,2048,512]{2,1,0:T(8,128)(2,1)} %all-gather.8.cloned.1.call-done, bf16[512,2048]{1,0:T(8,128)(2,1)} %all-gather.6.cloned.1.call-done, f32[2048]{0:T(1024)S(1)} %copy-done.14, f32[512]{0:T(512)S(1)} %add_rsqrt_fusion.1), kind=kOutput, calls=%fused_computation.11 | convolution fusion | flops 4299161600 | bytes 14690304 | tf_op jit(solution)/shard_map/rd,bdc->brc/dot_general | solution.py:107
  251.3 1.3 fusion.87
  252.6 1.1 slice.202
  253.7 0.9 slice_bitcast_fusion.9
  254.6 1.6 squeeze.52
  256.2 1.4 squeeze.51
  257.5 2.0 copy.62
  259.5 1.9 collective-permute-start.5
  261.4 1.6 squeeze.44
  263.0 2.0 convert_element_type.130
  264.9 1.9 copy.52
  266.9 1.6 slice_bitcast_fusion.3
  268.4 3.3 collective-permute-start
  271.7 1.9 pad_maximum_fusion.2
  273.6 2.0 concatenate.90
  275.5 1.1 copy.61
  276.7 2.8 fusion.41
  280.2 1.4 fusion.18
  281.5 0.8 copy-done.6
  283.0 2.7 collective-permute-start.6
  285.7 0.8 pad_maximum_fusion.5
  286.5 2.0 concatenate.77
  288.5 1.1 copy.51
  289.7 2.4 fusion.43
  293.1 1.8 pad_maximum_fusion.1
  294.9 1.9 concatenate.94
  296.8 1.1 copy.65
  298.0 2.5 fusion.40
  301.1 1.4 fusion.17
  302.5 3.9 %collective-permute-start.7 = (bf16[128,512]{1,0:T(8,128)(2,1)S(1)}, bf16[128,512]{1,0:T(8,128)(2,1)S(1)}, u32[]{:S(2)}, u32[]{:S(2)}) collective-permute-start(bf16[128,512]{1,0:T(8,128)(2,1)S(1)} %slice.179), channel_id=1, source_target_pairs={{0,4},{4,8},{8,12},{1,5},{5,9},{9,13},{2,6},{6,10},{10,14},{3,7},{... | collective-permute-start | bytes 393224 | tf_op jit(solution)/shard_map/ppermute | solution.py:20
  306.5 1.4 fusion.21
  308.5 3.0 collective-permute-start.1
  311.8 1.6 convolution_bitcast_fusion.6
  313.9 2.2 fusion.16
  317.4 2.3 fusion.42
  320.4 7.7 %collective-permute-done.8 = bf16[512,512]{1,0:T(8,128)(2,1)} collective-permute-done((bf16[512,512]{1,0:T(8,128)(2,1)}, bf16[512,512]{1,0:T(8,128)(2,1)}, u32[]{:S(2)}, u32[]{:S(2)}) %collective-permute-start.8) | collective-permute-done | bytes 524320 | tf_op jit(solution)/shard_map/ppermute | solution.py:14
  328.1 1.4 fusion.20
  329.5 2.3 collective-permute-start.2
  331.8 8.1 %collective-permute-done.2 = bf16[128,512]{1,0:T(8,128)(2,1)S(1)} collective-permute-done((bf16[128,512]{1,0:T(8,128)(2,1)S(1)}, bf16[128,512]{1,0:T(8,128)(2,1)S(1)}, u32[]{:S(2)}, u32[]{:S(2)}) %collective-permute-start.2) | collective-permute-done | bytes 131104 | tf_op jit(solution)/shard_map/ppermute | solution.py:20
  340.1 1.6 convolution_bitcast_fusion.7
  342.2 9.0 %collective-permute-done.9 = bf16[512,512]{1,0:T(8,128)(2,1)S(1)} collective-permute-done((bf16[512,512]{1,0:T(8,128)(2,1)}, bf16[512,512]{1,0:T(8,128)(2,1)S(1)}, u32[]{:S(2)}, u32[]{:S(2)}) %collective-permute-start.9) | collective-permute-done | bytes 524320 | tf_op jit(solution)/shard_map/ppermute | solution.py:14
  351.8 2.3 add_convert_fusion
  354.2 25.4 %all-gather.12.cloned.1.call-done = bf16[512,2048]{1,0:T(8,128)(2,1)} async-done(((bf16[512,512]{1,0:T(8,128)(2,1)}), bf16[512,2048]{1,0:T(8,128)(2,1)}) %all-gather.12.cloned.1.call-update) | async-done | bytes 2097168 | tf_op jit(solution)/shard_map/all_gather | solution.py:130
  379.6 4.3 %convolution_convert_fusion = bf16[512,512]{1,0:T(8,128)(2,1)} fusion(bf16[512,2048]{1,0:T(8,128)(2,1)} %all-gather.12.cloned.1.call-done, bf16[2048,512]{1,0:T(8,128)(2,1)} %all-gather.14.cloned.1.call-done), kind=kOutput, calls=%fused_computation.28 | convolution fusion | flops 1074003968 | bytes 4718592 | tf_op jit(solution)/shard_map/dot_general | solution.py:131
  (102 shorter events, 13.9 us)
Async XLA Ops:
  6.5 0.7 copy-start
  6.5 58.2 %all-gather.6.cloned.1.call-start = ((), (), s32[]{:S(2)}) async-start(), calls=%async_computation | async-start | bytes 2621440 | tf_op jit(solution)/shard_map/all_gather | solution.py:101
  9.4 71.0 %all-gather.10.cloned.1.call-start = ((), (), s32[]{:S(2)}) async-start(), calls=%async_computation.2 | async-start | bytes 2621440 | tf_op jit(solution)/shard_map/all_gather | solution.py:102
  11.2 46.9 %copy-start.13 = (s32[16]{0:T(128)S(1)}, s32[16]{0:T(128)}, u32[]{:S(2)}) copy-start(s32[16]{0:T(128)} %param.14) | copy-start | bytes 196
  11.2 47.1 %copy-start.12 = (f32[3,4,128]{2,1,0:T(4,128)S(1)}, f32[3,4,128]{2,1,0:T(4,128)}, u32[]{:S(2)}) copy-start(f32[3,4,128]{2,1,0:T(4,128)} %param.18) | copy-start | bytes 18436
  11.2 15.0 %collective-permute-start.3 = (bf16[512,512]{1,0:T(8,128)(2,1)S(1)}, bf16[512,512]{1,0:T(8,128)(2,1)S(1)}, u32[]{:S(2)}, u32[]{:S(2)}) collective-permute-start(bf16[512,512]{1,0:T(8,128)(2,1)S(1)} %fusion.15), channel_id=1, source_target_pairs={{0,4},{4,0},{8,12},{12,8},{1,5},{5,1},{9,13},{13,9},{2,6},{6,2},{1... | collective-permute-start | bytes 1572872 | tf_op jit(solution)/shard_map/ppermute | solution.py:14
  26.2 25.3 %collective-permute-start.4 = (bf16[512,512]{1,0:T(8,128)(2,1)S(1)}, bf16[512,512]{1,0:T(8,128)(2,1)S(1)}, u32[]{:S(2)}, u32[]{:S(2)}) collective-permute-start(bf16[512,512]{1,0:T(8,128)(2,1)S(1)} %collective-permute-done.3), channel_id=1, source_target_pairs={{0,8},{8,0},{4,12},{12,4},{1,9},{9,1},{5,13},{13,5},{2,10},{10,2},... | collective-permute-start | bytes 1572872 | tf_op jit(solution)/shard_map/ppermute | solution.py:14
  56.7 175.0 %all-gather.8.cloned.1.call-start = ((), (), s32[]{:S(2)}) async-start(), calls=%async_computation.1 | async-start | bytes 10485760 | tf_op jit(solution)/shard_map/all_gather | solution.py:106
  57.4 296.8 %all-gather.14.cloned.1.call-start = ((), (), s32[]{:S(2)}) async-start(), calls=%async_computation.4 | async-start | bytes 2621440 | tf_op jit(solution)/shard_map/all_gather | solution.py:133
  58.0 321.6 %all-gather.12.cloned.1.call-start = ((), (), s32[]{:S(2)}) async-start(), calls=%async_computation.3 | async-start | bytes 2621440 | tf_op jit(solution)/shard_map/all_gather | solution.py:130
  64.7 167.0 %copy-start.14 = (f32[2048]{0:T(1024)S(1)}, f32[2048]{0:T(1024)}, u32[]{:S(2)}) copy-start(f32[2048]{0:T(1024)} %param.16) | copy-start | bytes 24580
  80.4 151.3 %copy-start.10 = (bf16[512,2048]{1,0:T(8,128)(2,1)S(1)}, bf16[512,2048]{1,0:T(8,128)(2,1)}, u32[]{:S(2)}) copy-start(bf16[512,2048]{1,0:T(8,128)(2,1)} %all-gather.10.cloned.1.call-done) | copy-start | bytes 6291460
  238.7 2.3 copy-start.3
  251.3 2.5 copy-start.2
  259.5 12.2 %collective-permute-start.5 = (bf16[128,512]{1,0:T(8,128)(2,1)}, bf16[128,512]{1,0:T(8,128)(2,1)}, u32[]{:S(2)}, u32[]{:S(2)}) collective-permute-start(bf16[128,512]{1,0:T(8,128)(2,1)} %slice_bitcast_fusion.2), channel_id=1, source_target_pairs={{0,4},{4,8},{8,12},{1,5},{5,9},{9,13},{2,6},{6,10},{10,14},{3,7},{... | collective-permute-start | bytes 393224 | tf_op jit(solution)/shard_map/ppermute | solution.py:20
  268.4 17.3 %collective-permute-start = (bf16[128,512]{1,0:T(8,128)(2,1)}, bf16[128,512]{1,0:T(8,128)(2,1)S(1)}, u32[]{:S(2)}, u32[]{:S(2)}) collective-permute-start(bf16[128,512]{1,0:T(8,128)(2,1)} %slice_bitcast_fusion.3), channel_id=1, source_target_pairs={{0,4},{4,8},{8,12},{1,5},{5,9},{9,13},{2,6},{6,10},{10,14},{3,7},{... | collective-permute-start | bytes 393224 | tf_op jit(solution)/shard_map/ppermute | solution.py:20
  279.5 6.2 %copy-start.11 = (bf16[512,512]{1,0:T(8,128)(2,1)S(1)}, bf16[512,512]{1,0:T(8,128)(2,1)}, u32[]{:S(2)}) copy-start(bf16[512,512]{1,0:T(8,128)(2,1)} %slice_bitcast_fusion.9) | copy-start | bytes 1572868
  281.5 0.8 copy-start.6
  283.0 9.7 %collective-permute-start.6 = (bf16[128,512]{1,0:T(8,128)(2,1)}, bf16[128,512]{1,0:T(8,128)(2,1)}, u32[]{:S(2)}, u32[]{:S(2)}) collective-permute-start(bf16[128,512]{1,0:T(8,128)(2,1)} %slice.178), channel_id=1, source_target_pairs={{0,4},{4,8},{8,12},{1,5},{5,9},{9,13},{2,6},{6,10},{10,14},{3,7},{... | collective-permute-start | bytes 393224 | tf_op jit(solution)/shard_map/ppermute | solution.py:20
  292.1 1.0 copy-start.7
  302.5 9.0 %collective-permute-start.7 = (bf16[128,512]{1,0:T(8,128)(2,1)S(1)}, bf16[128,512]{1,0:T(8,128)(2,1)S(1)}, u32[]{:S(2)}, u32[]{:S(2)}) collective-permute-start(bf16[128,512]{1,0:T(8,128)(2,1)S(1)} %slice.179), channel_id=1, source_target_pairs={{0,4},{4,8},{8,12},{1,5},{5,9},{9,13},{2,6},{6,10},{10,14},{3,7},{... | collective-permute-start | bytes 393224 | tf_op jit(solution)/shard_map/ppermute | solution.py:20
  307.8 3.9 %copy-start.4 = (bf16[512,512]{1,0:T(8,128)(2,1)}, bf16[512,512]{1,0:T(8,128)(2,1)S(1)}, u32[]{:S(2)}) copy-start(bf16[512,512]{1,0:T(8,128)(2,1)S(1)} %fusion.21) | copy-start | bytes 1572868
  307.9 3.9 %copy-start.9 = (bf16[4,128,256]{2,1,0:T(8,128)(2,1)S(1)}, bf16[4,128,256]{2,1,0:T(8,128)(2,1)}, u32[]{:S(2)}) copy-start(bf16[4,128,256]{2,1,0:T(8,128)(2,1)} %compare_convert_fusion) | copy-start | bytes 786436
  308.5 7.9 %collective-permute-start.1 = (bf16[128,512]{1,0:T(8,128)(2,1)}, bf16[128,512]{1,0:T(8,128)(2,1)S(1)}, u32[]{:S(2)}, u32[]{:S(2)}) collective-permute-start(bf16[128,512]{1,0:T(8,128)(2,1)} %slice.169), channel_id=1, source_target_pairs={{0,4},{4,8},{8,12},{1,5},{5,9},{9,13},{2,6},{6,10},{10,14},{3,7},{... | collective-permute-start | bytes 393224 | tf_op jit(solution)/shard_map/ppermute | solution.py:20
  313.8 2.6 copy-start.5
  316.1 12.0 %collective-permute-start.8 = (bf16[512,512]{1,0:T(8,128)(2,1)}, bf16[512,512]{1,0:T(8,128)(2,1)}, u32[]{:S(2)}, u32[]{:S(2)}) collective-permute-start(bf16[512,512]{1,0:T(8,128)(2,1)} %fusion.16), channel_id=1, source_target_pairs={{0,4},{4,0},{8,12},{12,8},{1,5},{5,1},{9,13},{13,9},{2,6},{6,2},{1... | collective-permute-start | bytes 1572872 | tf_op jit(solution)/shard_map/ppermute | solution.py:14
  316.5 1.0 copy-start.8
  328.1 23.1 %collective-permute-start.9 = (bf16[512,512]{1,0:T(8,128)(2,1)}, bf16[512,512]{1,0:T(8,128)(2,1)S(1)}, u32[]{:S(2)}, u32[]{:S(2)}) collective-permute-start(bf16[512,512]{1,0:T(8,128)(2,1)} %collective-permute-done.8), channel_id=1, source_target_pairs={{0,8},{8,0},{4,12},{12,4},{1,9},{9,1},{5,13},{13,5},{2,10},{10,2},... | collective-permute-start | bytes 1572872 | tf_op jit(solution)/shard_map/ppermute | solution.py:14
  329.5 10.4 %collective-permute-start.2 = (bf16[128,512]{1,0:T(8,128)(2,1)S(1)}, bf16[128,512]{1,0:T(8,128)(2,1)S(1)}, u32[]{:S(2)}, u32[]{:S(2)}) collective-permute-start(bf16[128,512]{1,0:T(8,128)(2,1)S(1)} %slice.170), channel_id=1, source_target_pairs={{0,4},{4,8},{8,12},{1,5},{5,9},{9,13},{2,6},{6,10},{10,14},{3,7},{... | collective-permute-start | bytes 393224 | tf_op jit(solution)/shard_map/ppermute | solution.py:20
  354.2 29.7 %copy-start.1 = (bf16[4,512]{1,0:T(4,128)(2,1)S(1)}, bf16[4,512]{1,0:T(4,128)(2,1)}, u32[]{:S(2)}) copy-start(bf16[4,512]{1,0:T(4,128)(2,1)} %param.15) | copy-start | bytes 12292
Sparse Core Ops, SparseCore 0:
  9.6 25.2 all-gather.5
  56.8 23.5 all-gather.9
  82.0 149.6 all-gather.7
  233.1 46.2 all-gather.13
  354.3 25.2 all-gather.11
where the time goes:
time: 392 us; the launch traced here: 390 us
  waiting for transfers between devices  248 us (63%)
  local copies, waits for them, and re-layouts  48.7 us (12%)
  matrix products  36.2 us (9%)
  starting transfers between devices  23.1 us (6%)
  other arithmetic  20.5 us (5%)
  between operations  13.7 us (3%)
    all_gather x1, waiting for transfers between devices, local(): piece = lax.all_gather(in_weight, 'ctx', axis=1, tiled=True)  149 us
    ppermute x4, waiting for transfers between devices, partner(): return lax.ppermute(block, axis, route)  51.2 us
    all_gather x1, waiting for transfers between devices, local(): whole_sum = lax.all_gather(mixed_sum, 'ch', axis=1, tiled=True)  25.4 us
    ppermute x6, starting transfers between devices, shifted(): return lax.ppermute(value, axis, pairs)  17.1 us
    all_gather x1, waiting for transfers between devices, local(): lax.all_gather(rev_input, 'ch', axis=1, tiled=True)  13.3 us
    dot_general x6, matrix products, blockwise_conv(): jnp.einsum('nhts,nshd->nthd', kernel, window, preferred_element_type=jnp....  13.2 us
    concatenate x12, local copies, waits for them, and re-layouts, blockwise_conv(): jnp.concatenate([extended[:rows].reshape(blocks, block, width), extended[...  9.97 us
    ppermute x6, waiting for transfers between devices, shifted(): return lax.ppermute(value, axis, pairs)  8.09 us
  transfers between devices with their start and end apart: 15, of which 8 were waited for; matrix products, arithmetic and copies ran while one was open for 24% of the time, Pallas kernels for 0%

commit v1 on v0

--- a/solution.py
+++ b/solution.py
@@ -2,6 +2,19 @@
 import jax.numpy as jnp
 from jax import lax
 from jax.sharding import PartitionSpec as P
+
+
+def gather_around(shard, axis, dim):
+    ways = lax.axis_size(axis)
+    up = [(d, (d + 1) % ways) for d in range(ways)]
+    down = [(d, (d - 1) % ways) for d in range(ways)]
+    earlier, later = ([shard], [shard])
+    for _ in range(ways // 2):
+        earlier.append(lax.ppermute(earlier[-1], axis, up))
+    for _ in range((ways - 1) // 2):
+        later.append(lax.ppermute(later[-1], axis, down))
+    line = jnp.concatenate([*earlier[::-1], *later[1:]], axis=dim)
+    return jnp.roll(line, (lax.axis_index(axis) - ways // 2) * shard.shape[dim], axis=dim)
 
 
 def partner(block, axis, apart):
@@ -127,7 +140,7 @@
         mixed_rev = partner(mixed_rev, "ctx", level)
     mixed_rev = mixed_rev[::-1]
     mixed_sum = (mixed_fwd.astype(jnp.float32) + mixed_rev.astype(jnp.float32)).astype(jnp.bfloat16)
-    whole_sum = lax.all_gather(mixed_sum, "ch", axis=1, tiled=True)
+    whole_sum = gather_around(mixed_sum, "ch", 1)
     total = jnp.dot(
         whole_sum,
         lax.all_gather(out_weight, "ctx", axis=0, tiled=True),

time: 392 us -> 428 us (1.092); the launches traced: 390 us -> 422 us
  waiting for transfers between devices: 248 us -> 273 us
  local copies, waits for them, and re-layouts: 48.7 us -> 54.8 us
    all_gather x1 -> x0, waiting for transfers between devices: 25.4 us -> none  [local(): whole_sum = lax.all_gather(mixed_sum, 'ch', axis=1, tiled=True)]
    ppermute x0 -> x3, waiting for transfers between devices: none -> 18.6 us  [the longest x2 18.6 us: gather_around(): earlier.append(lax.ppermute(earlier[-1], axis, up))]
    ppermute x4, waiting for transfers between devices: 51.2 us -> 66.9 us  [partner(): return lax.ppermute(block, axis, route)]
    ppermute x6, waiting for transfers between devices: 8.09 us -> 23.5 us  [shifted(): return lax.ppermute(value, axis, pairs)]
    unnamed x33 -> x38, local copies, waits for them, and re-layouts: 5.73 us -> 10.1 us
  transfers between devices with their start and end apart: 15 -> 17, of which waited for: 8 -> 9; matrix products, arithmetic and copies ran while one was open for 24% -> 16% of each run, Pallas kernels for 0% -> 0%
where the time goes in v1:
time: 428 us; the launch traced here: 422 us
  waiting for transfers between devices  273 us (64%)
  local copies, waits for them, and re-layouts  54.8 us (13%)
  matrix products  37.9 us (9%)
  starting transfers between devices  22.4 us (5%)
  other arithmetic  20 us (5%)
  between operations  13.7 us (3%)
    all_gather x1, waiting for transfers between devices, local(): piece = lax.all_gather(in_weight, 'ctx', axis=1, tiled=True)  149 us
    ppermute x4, waiting for transfers between devices, partner(): return lax.ppermute(block, axis, route)  66.9 us
    ppermute x6, waiting for transfers between devices, shifted(): return lax.ppermute(value, axis, pairs)  23.5 us
    ppermute x2, waiting for transfers between devices, gather_around(): earlier.append(lax.ppermute(earlier[-1], axis, up))  18.6 us
    dot_general x6, matrix products, blockwise_conv(): jnp.einsum('nhts,nshd->nthd', kernel, window, preferred_element_type=jnp....  14.3 us
    all_gather x1, waiting for transfers between devices, local(): lax.all_gather(rev_input, 'ch', axis=1, tiled=True)  14.1 us
    ppermute x6, starting transfers between devices, shifted(): return lax.ppermute(value, axis, pairs)  13 us
    concatenate x12, local copies, waits for them, and re-layouts, blockwise_conv(): jnp.concatenate([extended[:rows].reshape(blocks, block, width), extended[...  10.1 us
  transfers between devices with their start and end apart: 17, of which 9 were waited for; matrix products, arithmetic and copies ran while one was open for 16% of the time, Pallas kernels for 0%

profile of v1, /device:TPU:0, one launch (start us, length us, event | category | flops | bytes accessed | tf_op | source)
XLA Modules:
  0.0 421.8 jit_solution(159476866805656895)
XLA Ops:
  7.2 2.2 fusion.16
  9.5 1.7 fusion.17
  11.2 3.1 collective-permute-start.3
  14.2 11.9 %collective-permute-done.3 = bf16[512,512]{1,0:T(8,128)(2,1)S(1)} collective-permute-done((bf16[512,512]{1,0:T(8,128)(2,1)S(1)}, bf16[512,512]{1,0:T(8,128)(2,1)S(1)}, u32[]{:S(2)}, u32[]{:S(2)}) %collective-permute-start.3) | collective-permute-done | bytes 524320 | tf_op jit(solution)/shard_map/ppermute | solution.py:27
  26.2 2.8 collective-permute-start.4
  28.9 22.6 %collective-permute-done.4 = bf16[512,512]{1,0:T(8,128)(2,1)S(1)} collective-permute-done((bf16[512,512]{1,0:T(8,128)(2,1)S(1)}, bf16[512,512]{1,0:T(8,128)(2,1)S(1)}, u32[]{:S(2)}, u32[]{:S(2)}) %collective-permute-start.4) | collective-permute-done | bytes 524320 | tf_op jit(solution)/shard_map/ppermute | solution.py:27
  51.5 5.1 %rev.21 = bf16[512,512]{1,0:T(8,128)(2,1)} reverse(bf16[512,512]{1,0:T(8,128)(2,1)S(1)} %collective-permute-done.4), dimensions={0} | reverse | bytes 1048576 | tf_op jit(solution)/shard_map/rev | solution.py:112
  64.1 2.2 fusion
  66.3 14.1 %all-gather.9.cloned.1.call-done = bf16[512,2048]{1,0:T(8,128)(2,1)} async-done(((bf16[512,512]{1,0:T(8,128)(2,1)}), bf16[512,2048]{1,0:T(8,128)(2,1)}) %all-gather.9.cloned.1.call-update) | async-done | bytes 2097168 | tf_op jit(solution)/shard_map/all_gather | solution.py:115
  80.4 2.1 fusion.3
  82.5 149.2 %all-gather.7.cloned.1.call-done = bf16[4,2048,512]{2,1,0:T(8,128)(2,1)} async-done(((bf16[4,512,512]{2,1,0:T(8,128)(2,1)}), bf16[4,2048,512]{2,1,0:T(8,128)(2,1)}) %all-gather.7.cloned.1.call-update) | async-done | bytes 8388624 | tf_op jit(solution)/shard_map/all_gather | solution.py:119
  231.6 7.7 %convolution_bitcast_fusion = f32[4,512,512]{2,1,0:T(8,128)S(1)} fusion(bf16[4,2048,512]{2,1,0:T(8,128)(2,1)} %all-gather.7.cloned.1.call-done, bf16[512,2048]{1,0:T(8,128)(2,1)} %all-gather.9.cloned.1.call-done, f32[512]{0:T(512)S(1)} %add_rsqrt_fusion, f32[2048]{0:T(1024)S(1)} %copy-done.13), kind=kOutput, calls=%fused_computation.10 | convolution fusion | flops 4299161600 | bytes 14690304 | tf_op jit(solution)/shard_map/rd,bdc->brc/dot_general | solution.py:121
  239.4 1.3 fusion.94
  240.8 0.9 copy-done.3
  242.6 0.9 convert_element_type.147
  244.2 7.7 %convolution_bitcast_fusion.1 = f32[4,512,512]{2,1,0:T(8,128)S(1)} fusion(bf16[4,2048,512]{2,1,0:T(8,128)(2,1)} %all-gather.7.cloned.1.call-done, bf16[512,2048]{1,0:T(8,128)(2,1)} %all-gather.5.cloned.1.call-done, f32[2048]{0:T(1024)S(1)} %copy-done.13, f32[512]{0:T(512)S(1)} %add_rsqrt_fusion.1), kind=kOutput, calls=%fused_computation.11 | convolution fusion | flops 4299161600 | bytes 14690304 | tf_op jit(solution)/shard_map/rd,bdc->brc/dot_general | solution.py:120
  251.9 1.3 fusion.93
  253.2 1.1 slice.202
  255.2 1.6 squeeze.52
  256.7 1.4 squeeze.51
  258.1 2.0 copy.62
  260.0 1.9 collective-permute-start.5
  262.0 1.6 squeeze.44
  263.6 2.0 convert_element_type.130
  265.5 1.9 copy.52
  267.4 1.6 slice_bitcast_fusion.3
  269.0 3.2 collective-permute-start
  272.3 1.9 pad_maximum_fusion.2
  274.1 2.0 concatenate.96
  276.1 1.1 copy.61
  277.3 2.8 fusion.46
  280.8 1.4 fusion.23
  283.6 2.7 collective-permute-start.6
  287.2 2.0 concatenate.83
  289.2 1.2 copy.51
  290.4 2.5 fusion.48
  293.6 1.7 pad_maximum_fusion.1
  295.3 2.0 concatenate.100
  297.3 1.1 copy.65
  298.4 2.4 fusion.45
  301.5 1.4 fusion.22
  302.9 1.4 collective-permute-start.7
  304.3 1.4 fusion.26
  305.8 1.9 collective-permute-start.1
  308.0 2.6 convolution_bitcast_fusion.6
  310.6 1.7 copy.70
  312.3 2.2 fusion.21
  314.5 1.6 collective-permute-start.8
  316.8 2.4 fusion.47
  319.9 15.2 %collective-permute-done.8 = bf16[512,512]{1,0:T(8,128)(2,1)} collective-permute-done((bf16[512,512]{1,0:T(8,128)(2,1)}, bf16[512,512]{1,0:T(8,128)(2,1)}, u32[]{:S(2)}, u32[]{:S(2)}) %collective-permute-start.8) | collective-permute-done | bytes 524320 | tf_op jit(solution)/shard_map/ppermute | solution.py:27
  335.2 1.4 fusion.25
  336.6 1.8 collective-permute-start.2
  338.3 23.5 %collective-permute-done.2 = bf16[128,512]{1,0:T(8,128)(2,1)S(1)} collective-permute-done((bf16[128,512]{1,0:T(8,128)(2,1)S(1)}, bf16[128,512]{1,0:T(8,128)(2,1)S(1)}, u32[]{:S(2)}, u32[]{:S(2)}) %collective-permute-start.2) | collective-permute-done | bytes 131104 | tf_op jit(solution)/shard_map/ppermute | solution.py:33
  362.1 1.6 convolution_bitcast_fusion.7
  364.2 17.2 %collective-permute-done.9 = bf16[512,512]{1,0:T(8,128)(2,1)S(1)} collective-permute-done((bf16[512,512]{1,0:T(8,128)(2,1)}, bf16[512,512]{1,0:T(8,128)(2,1)S(1)}, u32[]{:S(2)}, u32[]{:S(2)}) %collective-permute-start.9) | collective-permute-done | bytes 524320 | tf_op jit(solution)/shard_map/ppermute | solution.py:27
  381.9 1.6 add_convert_fusion
  383.6 8.6 %collective-permute-done.10 = bf16[512,512]{1,0:T(8,128)(2,1)S(1)} collective-permute-done((bf16[512,512]{1,0:T(8,128)(2,1)S(1)}, bf16[512,512]{1,0:T(8,128)(2,1)S(1)}, u32[]{:S(2)}, u32[]{:S(2)}) %collective-permute-start.10) | collective-permute-done | bytes 524320 | tf_op jit(solution)/shard_map/ppermute | solution.py:13
  392.2 1.7 collective-permute-start.12
  393.9 10.0 %collective-permute-done.11 = bf16[512,512]{1,0:T(8,128)(2,1)S(1)} collective-permute-done((bf16[512,512]{1,0:T(8,128)(2,1)S(1)}, bf16[512,512]{1,0:T(8,128)(2,1)S(1)}, u32[]{:S(2)}, u32[]{:S(2)}) %collective-permute-start.11) | collective-permute-done | bytes 524320 | tf_op jit(solution)/shard_map/ppermute | solution.py:13
  403.9 0.9 constant_dynamic-update-slice_fusion.7
  404.8 0.9 constant_dynamic-update-slice_fusion.6
  409.2 0.9 constant_dynamic-update-slice_fusion.1
  410.1 0.9 constant_dynamic-update-slice_fusion
  411.0 4.3 %fusion.18 = bf16[512,512]{1,0:T(8,128)(2,1)} fusion(bf16[2048,512]{1,0:T(8,128)(2,1)} %all-gather.11.cloned.1.call-done, bf16[512,4096]{1,0:T(8,128)(2,1)} %constant_dynamic-update-slice_fusion, s32[]{:T(128)S(6)} %select_n.47), kind=kOutput, calls=%fused_computation.30 | convolution fusion | flops 1074003968 | bytes 4718596 | tf_op jit(solution)/shard_map/dot_general | solution.py:144
  (111 shorter events, 21.3 us)
Async XLA Ops:
  6.5 0.7 copy-start
  6.5 50.9 %copy-start.11 = (f32[3,4,128]{2,1,0:T(4,128)S(1)}, f32[3,4,128]{2,1,0:T(4,128)}, u32[]{:S(2)}) copy-start(f32[3,4,128]{2,1,0:T(4,128)} %param.18) | copy-start | bytes 18436
  6.5 57.6 %all-gather.5.cloned.1.call-start = ((), (), s32[]{:S(2)}) async-start(), calls=%async_computation | async-start | bytes 2621440 | tf_op jit(solution)/shard_map/all_gather | solution.py:114
  9.4 70.9 %all-gather.9.cloned.1.call-start = ((), (), s32[]{:S(2)}) async-start(), calls=%async_computation.2 | async-start | bytes 2621440 | tf_op jit(solution)/shard_map/all_gather | solution.py:115
  11.2 15.0 %collective-permute-start.3 = (bf16[512,512]{1,0:T(8,128)(2,1)S(1)}, bf16[512,512]{1,0:T(8,128)(2,1)S(1)}, u32[]{:S(2)}, u32[]{:S(2)}) collective-permute-start(bf16[512,512]{1,0:T(8,128)(2,1)S(1)} %fusion.17), channel_id=1, source_target_pairs={{0,4},{4,0},{8,12},{12,8},{1,5},{5,1},{9,13},{13,9},{2,6},{6,2},{1... | collective-permute-start | bytes 1572872 | tf_op jit(solution)/shard_map/ppermute | solution.py:27
  26.2 25.3 %collective-permute-start.4 = (bf16[512,512]{1,0:T(8,128)(2,1)S(1)}, bf16[512,512]{1,0:T(8,128)(2,1)S(1)}, u32[]{:S(2)}, u32[]{:S(2)}) collective-permute-start(bf16[512,512]{1,0:T(8,128)(2,1)S(1)} %collective-permute-done.3), channel_id=1, source_target_pairs={{0,8},{8,0},{4,12},{12,4},{1,9},{9,1},{5,13},{13,5},{2,10},{10,2},... | collective-permute-start | bytes 1572872 | tf_op jit(solution)/shard_map/ppermute | solution.py:27
  56.7 5.6 %copy-start.12 = (s32[16]{0:T(128)S(1)}, s32[16]{0:T(128)}, u32[]{:S(2)}) copy-start(s32[16]{0:T(128)} %param.14) | copy-start | bytes 196
  56.7 175.0 %all-gather.7.cloned.1.call-start = ((), (), s32[]{:S(2)}) async-start(), calls=%async_computation.1 | async-start | bytes 10485760 | tf_op jit(solution)/shard_map/all_gather | solution.py:119
  57.4 353.6 %all-gather.11.cloned.1.call-start = ((), (), s32[]{:S(2)}) async-start(), calls=%async_computation.3 | async-start | bytes 2621440 | tf_op jit(solution)/shard_map/all_gather | solution.py:146
  59.7 172.0 %copy-start.13 = (f32[2048]{0:T(1024)S(1)}, f32[2048]{0:T(1024)}, u32[]{:S(2)}) copy-start(f32[2048]{0:T(1024)} %param.16) | copy-start | bytes 24580
  239.4 2.3 copy-start.3
  251.9 2.4 copy-start.2
  260.0 12.2 %collective-permute-start.5 = (bf16[128,512]{1,0:T(8,128)(2,1)}, bf16[128,512]{1,0:T(8,128)(2,1)}, u32[]{:S(2)}, u32[]{:S(2)}) collective-permute-start(bf16[128,512]{1,0:T(8,128)(2,1)} %slice_bitcast_fusion.2), channel_id=1, source_target_pairs={{0,4},{4,8},{8,12},{1,5},{5,9},{9,13},{2,6},{6,10},{10,14},{3,7},{... | collective-permute-start | bytes 393224 | tf_op jit(solution)/shard_map/ppermute | solution.py:33
  269.0 17.4 %collective-permute-start = (bf16[128,512]{1,0:T(8,128)(2,1)}, bf16[128,512]{1,0:T(8,128)(2,1)S(1)}, u32[]{:S(2)}, u32[]{:S(2)}) collective-permute-start(bf16[128,512]{1,0:T(8,128)(2,1)} %slice_bitcast_fusion.3), channel_id=1, source_target_pairs={{0,4},{4,8},{8,12},{1,5},{5,9},{9,13},{2,6},{6,10},{10,14},{3,7},{... | collective-permute-start | bytes 393224 | tf_op jit(solution)/shard_map/ppermute | solution.py:33
  277.3 9.1 %copy-start.10 = (bf16[512,512]{1,0:T(8,128)(2,1)S(1)}, bf16[512,512]{1,0:T(8,128)(2,1)}, u32[]{:S(2)}) copy-start(bf16[512,512]{1,0:T(8,128)(2,1)} %slice_bitcast_fusion.9) | copy-start | bytes 1572868
  282.2 0.8 copy-start.6
  283.6 9.9 %collective-permute-start.6 = (bf16[128,512]{1,0:T(8,128)(2,1)}, bf16[128,512]{1,0:T(8,128)(2,1)}, u32[]{:S(2)}, u32[]{:S(2)}) collective-permute-start(bf16[128,512]{1,0:T(8,128)(2,1)} %slice.178), channel_id=1, source_target_pairs={{0,4},{4,8},{8,12},{1,5},{5,9},{9,13},{2,6},{6,10},{10,14},{3,7},{... | collective-permute-start | bytes 393224 | tf_op jit(solution)/shard_map/ppermute | solution.py:33
  289.2 4.4 %copy-start.7 = (bf16[512,512]{1,0:T(8,128)(2,1)S(1)}, bf16[512,512]{1,0:T(8,128)(2,1)}, u32[]{:S(2)}) copy-start(bf16[512,512]{1,0:T(8,128)(2,1)} %copy-done.6) | copy-start | bytes 1572868
  302.9 5.1 %copy-start.9 = (bf16[4,128,256]{2,1,0:T(8,128)(2,1)S(1)}, bf16[4,128,256]{2,1,0:T(8,128)(2,1)}, u32[]{:S(2)}) copy-start(bf16[4,128,256]{2,1,0:T(8,128)(2,1)} %compare_convert_fusion) | copy-start | bytes 786436
  302.9 4.8 %collective-permute-start.7 = (bf16[128,512]{1,0:T(8,128)(2,1)S(1)}, bf16[128,512]{1,0:T(8,128)(2,1)S(1)}, u32[]{:S(2)}, u32[]{:S(2)}) collective-permute-start(bf16[128,512]{1,0:T(8,128)(2,1)S(1)} %slice.179), channel_id=1, source_target_pairs={{0,4},{4,8},{8,12},{1,5},{5,9},{9,13},{2,6},{6,10},{10,14},{3,7},{... | collective-permute-start | bytes 393224 | tf_op jit(solution)/shard_map/ppermute | solution.py:33
  305.7 2.2 copy-start.4
  305.8 10.8 %collective-permute-start.1 = (bf16[128,512]{1,0:T(8,128)(2,1)S(1)}, bf16[128,512]{1,0:T(8,128)(2,1)S(1)}, u32[]{:S(2)}, u32[]{:S(2)}) collective-permute-start(bf16[128,512]{1,0:T(8,128)(2,1)S(1)} %slice.169), channel_id=1, source_target_pairs={{0,4},{4,8},{8,12},{1,5},{5,9},{9,13},{2,6},{6,10},{10,14},{3,7},{... | collective-permute-start | bytes 393224 | tf_op jit(solution)/shard_map/ppermute | solution.py:33
  310.6 5.9 %copy-start.5 = (bf16[512,512]{1,0:T(8,128)(2,1)S(1)}, bf16[512,512]{1,0:T(8,128)(2,1)}, u32[]{:S(2)}) copy-start(bf16[512,512]{1,0:T(8,128)(2,1)} %copy-done.4) | copy-start | bytes 1572868
  312.3 4.5 %copy-start.8 = (bf16[4,128,256]{2,1,0:T(8,128)(2,1)S(1)}, bf16[4,128,256]{2,1,0:T(8,128)(2,1)}, u32[]{:S(2)}) copy-start(bf16[4,128,256]{2,1,0:T(8,128)(2,1)} %compare_convert_fusion.1) | copy-start | bytes 786436
  314.5 20.6 %collective-permute-start.8 = (bf16[512,512]{1,0:T(8,128)(2,1)}, bf16[512,512]{1,0:T(8,128)(2,1)}, u32[]{:S(2)}, u32[]{:S(2)}) collective-permute-start(bf16[512,512]{1,0:T(8,128)(2,1)} %fusion.21), channel_id=1, source_target_pairs={{0,4},{4,0},{8,12},{12,8},{1,5},{5,1},{9,13},{13,9},{2,6},{6,2},{1... | collective-permute-start | bytes 1572872 | tf_op jit(solution)/shard_map/ppermute | solution.py:27
  335.2 46.2 %collective-permute-start.9 = (bf16[512,512]{1,0:T(8,128)(2,1)}, bf16[512,512]{1,0:T(8,128)(2,1)S(1)}, u32[]{:S(2)}, u32[]{:S(2)}) collective-permute-start(bf16[512,512]{1,0:T(8,128)(2,1)} %collective-permute-done.8), channel_id=1, source_target_pairs={{0,8},{8,0},{4,12},{12,4},{1,9},{9,1},{5,13},{13,5},{2,10},{10,2},... | collective-permute-start | bytes 1572872 | tf_op jit(solution)/shard_map/ppermute | solution.py:27
  336.6 25.3 %collective-permute-start.2 = (bf16[128,512]{1,0:T(8,128)(2,1)S(1)}, bf16[128,512]{1,0:T(8,128)(2,1)S(1)}, u32[]{:S(2)}, u32[]{:S(2)}) collective-permute-start(bf16[128,512]{1,0:T(8,128)(2,1)S(1)} %slice.170), channel_id=1, source_target_pairs={{0,4},{4,8},{8,12},{1,5},{5,9},{9,13},{2,6},{6,10},{10,14},{3,7},{... | collective-permute-start | bytes 393224 | tf_op jit(solution)/shard_map/ppermute | solution.py:33
  383.5 8.7 %collective-permute-start.10 = (bf16[512,512]{1,0:T(8,128)(2,1)S(1)}, bf16[512,512]{1,0:T(8,128)(2,1)S(1)}, u32[]{:S(2)}, u32[]{:S(2)}) collective-permute-start(bf16[512,512]{1,0:T(8,128)(2,1)S(1)} %add_convert_fusion), channel_id=1, source_target_pairs={{0,1},{1,2},{2,3},{3,0},{4,5},{5,6},{6,7},{7,4},{8,9},{9,10},{10,1... | collective-permute-start | bytes 1572872 | tf_op jit(solution)/shard_map/ppermute | solution.py:13
  392.2 11.8 %collective-permute-start.11 = (bf16[512,512]{1,0:T(8,128)(2,1)S(1)}, bf16[512,512]{1,0:T(8,128)(2,1)S(1)}, u32[]{:S(2)}, u32[]{:S(2)}) collective-permute-start(bf16[512,512]{1,0:T(8,128)(2,1)S(1)} %collective-permute-done.10), channel_id=1, source_target_pairs={{0,1},{1,2},{2,3},{3,0},{4,5},{5,6},{6,7},{7,4},{8,9},{9,10},{10,1... | collective-permute-start | bytes 1572872 | tf_op jit(solution)/shard_map/ppermute | solution.py:13
  392.2 14.5 %collective-permute-start.12 = (bf16[512,512]{1,0:T(8,128)(2,1)S(1)}, bf16[512,512]{1,0:T(8,128)(2,1)S(1)}, u32[]{:S(2)}, u32[]{:S(2)}) collective-permute-start(bf16[512,512]{1,0:T(8,128)(2,1)S(1)} %add_convert_fusion), channel_id=1, source_target_pairs={{0,3},{1,0},{2,1},{3,2},{4,7},{5,4},{6,5},{7,6},{8,11},{9,8},{10,9... | collective-permute-start | bytes 1572872 | tf_op jit(solution)/shard_map/ppermute | solution.py:15
  409.2 6.0 %copy-start.1 = (bf16[4,512]{1,0:T(4,128)(2,1)S(1)}, bf16[4,512]{1,0:T(4,128)(2,1)}, u32[]{:S(2)}) copy-start(bf16[4,512]{1,0:T(4,128)(2,1)} %param.15) | copy-start | bytes 12292
Sparse Core Ops, SparseCore 0:
  9.6 25.2 all-gather.4
  56.8 23.5 all-gather.8
  82.0 149.6 all-gather.6
  316.3 67.1 all-gather.10
